TPU v7x, 512 devices: a whole 4x4x16 slice. The times are simulated.
512 devices in a mesh: group: 4 (over x), shard: 32 (over z, y_hi), tensor: 4 (over y_lo, core).
Axes of the slice: x: 4, y: 4 (y_hi: 2, y_lo: 2; y = y_hi * 2 + y_lo), z: 16, core: 2. Of those that a mesh axis runs over, the one named last changes fastest.
Arguments:
- deltas: bfloat16 [4, 2048, 2048], P('group', None, 'tensor'), may hold values from -6 to 6
- factor: bfloat16 [2048, 64], P('tensor'), may hold values from -0.29882812 to 0.29882812
- master: float32 [2048, 2048], P(('group', 'shard'), 'tensor'), may hold values from -6 to 6
- momentum: float32 [2048, 2048], P(('group', 'shard'), 'tensor'), may hold values from -3 to 3
Outputs:
- new_master: float32 [2048, 2048], P(('group', 'shard'), 'tensor')
- new_momentum: float32 [2048, 2048], P(('group', 'shard'), 'tensor')
- weights: bfloat16 [2048, 2048], P(None, 'tensor')
All inputs are finite; a program needn't handle non-finite values.
Results may differ from a plain program's by a relative error of at most 0.009.
Values may be sent and summed in bfloat16 or wider, within the bound.
A program may use at most 64 MiB of HBM per device.

v0:
```python
import jax
import jax.numpy as jnp
from jax import lax
from jax.sharding import PartitionSpec as P

momentum_rate = 0.9
outer_rate = 0.7


def shards(deltas, factor, master, momentum):
    group_count = lax.axis_size("group")
    shard_count = lax.axis_size("shard")
    shard_index = lax.axis_index("shard")
    row_count = master.shape[0]
    col_count = master.shape[1]
    own_delta = deltas[0]
    blocks = own_delta.reshape(group_count, shard_count, row_count, col_count)
    picked = lax.dynamic_index_in_dim(blocks, shard_index, 1, keepdims=False)
    factor_wide = factor.astype(jnp.float32)
    summed = lax.psum_scatter(
        picked.astype(jnp.float32).astype(jnp.bfloat16), "group", scatter_dimension=0, tiled=True
    ).astype(jnp.float32)
    partial_value = jnp.dot(summed[0], factor_wide, precision=lax.Precision.HIGHEST)
    coefficients = lax.psum(partial_value, "tensor")
    outer_grad = (
        lax.dot_general(
            coefficients, factor_wide, (((1,), (1,)), ((), ())), precision=lax.Precision.HIGHEST
        )
        / group_count
    )
    new_momentum = momentum_rate * momentum + outer_grad
    new_master = master - outer_rate * (outer_grad + momentum_rate * new_momentum)
    fresh_copy = new_master.astype(jnp.bfloat16)
    weights = lax.all_gather(fresh_copy, ("group", "shard"), axis=0, tiled=True)
    return (new_master, new_momentum, weights)


def solution(mesh):
    return jax.shard_map(
        shards,
        mesh=mesh,
        in_specs=(
            P("group", None, "tensor"),
            P("tensor", None),
            P(("group", "shard"), "tensor"),
            P(("group", "shard"), "tensor"),
        ),
        out_specs=(
            P(("group", "shard"), "tensor"),
            P(("group", "shard"), "tensor"),
            P(None, "tensor"),
        ),
        check_vma=False,
    )
```

profile of v0, /device:TPU:2, one launch (start us, length us, event | category | flops | bytes accessed | tf_op | source)
XLA Modules:
  0.0 274.1 jit_solution(17234697237845103731)
XLA Ops:
  7.2 0.0 copy-start
  7.2 0.0 reduce-scatter.2.cloned.1.call-start
  7.2 1.5 copy-done
  8.8 0.6 dynamic-slice_bitcast_fusion
  9.4 0.0 reduce-scatter.2.cloned.1.call-update
  9.4 0.0 all-gather.2.cloned.1.call-start
  9.5 33.2 %reduce-scatter.2.cloned.1.call-done = bf16[1,16,512]{2,1,0:T(8,128)(2,1)} async-done(((bf16[4,16,512]{2,1,0:T(8,128)(2,1)}), bf16[1,16,512]{2,1,0:T(8,128)(2,1)}) %reduce-scatter.2.cloned.1.call-update) | async-done | bytes 16400 | tf_op jit(solution)/shard_map/reduce_scatter | solution.py:20
  42.7 1.0 fusion
  43.7 5.7 %psum.7 = f32[16,64]{1,0:T(8,128)S(1)} all-reduce(f32[16,64]{1,0:T(8,128)S(1)} %fusion), channel_id=1, replica_groups=mesh['group'=4,'shard'=32,'tensor'=4] {'tensor'}, use_global_device_ids=true, to_apply=%region_1.2 | all-reduce | flops 1024 | bytes 8192 | tf_op jit(solution)/shard_map/psum | solution.py:24
  49.4 1.6 fusion.2
  51.1 0.0 all-gather.2.cloned.1.call-update
  51.1 213.1 %all-gather.2.cloned.1.call-done = bf16[2048,512]{1,0:T(8,128)(2,1)} async-done(((bf16[16,512]{1,0:T(8,128)(2,1)}), bf16[2048,512]{1,0:T(8,128)(2,1)}) %all-gather.2.cloned.1.call-update) | async-done | bytes 2097168 | tf_op jit(solution)/shard_map/all_gather | solution.py:34
  264.2 3.0 %copy.8 = bf16[2048,512]{1,0:T(8,128)(2,1)} copy(bf16[2048,512]{1,0:T(8,128)(2,1)} %all-gather.2.cloned.1.call-done) | data formatting | bytes 4194304
Async XLA Ops:
  7.2 1.6 copy-start
  7.2 35.5 %reduce-scatter.2.cloned.1.call-start = ((), (), s32[]{:S(2)}) async-start(), calls=%async_computation.1 | async-start | bytes 81920 | tf_op jit(solution)/shard_map/reduce_scatter | solution.py:20
  9.4 254.8 %all-gather.2.cloned.1.call-start = ((), (), s32[]{:S(2)}) async-start(), calls=%async_computation.2 | async-start | bytes 2113536 | tf_op jit(solution)/shard_map/all_gather | solution.py:34
Sparse Core Ops, SparseCore 0:
  11.4 31.2 reduce-scatter.1
  51.2 212.9 all-gather.1
where the time goes:
time: 274 us
  waiting for transfers between devices  246 us (90%)
  between operations  14.1 us (5%)
  blocking collectives  5.75 us (2%)
  local copies, waits for them, and re-layouts  5.22 us (2%)
    all_gather x1, waiting for transfers between devices, shards(): weights = lax.all_gather(fresh_copy, ('group', 'shard'), axis=0, tiled=True)  213 us
    reduce_scatter x1, waiting for transfers between devices, shards(): lax.psum_scatter(picked.astype(jnp.float32).astype(jnp.bfloat16), 'group'...  33.2 us
    psum x1, blocking collectives, shards(): coefficients = lax.psum(partial_value, 'tensor')  5.75 us
  transfers between devices with their start and end apart: 2, of which 2 were waited for; matrix products, arithmetic and copies ran while one was open for 0% of the time, Pallas kernels for 0%

commit v1 on v0

--- a/solution.py
+++ b/solution.py
@@ -31,7 +31,12 @@
     new_momentum = momentum_rate * momentum + outer_grad
     new_master = master - outer_rate * (outer_grad + momentum_rate * new_momentum)
     fresh_copy = new_master.astype(jnp.bfloat16)
-    weights = lax.all_gather(fresh_copy, ("group", "shard"), axis=0, tiled=True)
+    weights = jnp.concatenate(
+        lax.all_to_all(
+            jnp.stack([fresh_copy] * lax.axis_size(("group", "shard"))), ("group", "shard"), 0, 0
+        ),
+        axis=0,
+    )
     return (new_master, new_momentum, weights)
 
 

time: 274 us -> 179 us (0.65)
  waiting for transfers between devices: 246 us -> 33.3 us
  blocking collectives: 5.75 us -> 125 us
    all_gather x1 -> x0, waiting for transfers between devices: 213 us -> none  [shards(): weights = lax.all_gather(fresh_copy, ('group', 'shard'), axis=0, tiled=True)]
    all_to_all x0 -> x1, blocking collectives: none -> 119 us  [shards(): lax.all_to_all(jnp.stack([fresh_copy] * lax.axis_size(('group', 'shard'))...]
  transfers between devices with their start and end apart: 2 -> 1, of which waited for: 2 -> 1; matrix products, arithmetic and copies ran while one was open for 0% -> 0% of each run, Pallas kernels for 0% -> 0%
where the time goes in v1:
time: 179 us; the launch traced here: 178 us
  blocking collectives  125 us (70%)
  waiting for transfers between devices  33.3 us (19%)
  between operations  14.1 us (8%)
  local copies, waits for them, and re-layouts  3.74 us (2%)
  matrix products  2.62 us (1%)
    all_to_all x1, blocking collectives, shards(): lax.all_to_all(jnp.stack([fresh_copy] * lax.axis_size(('group', 'shard'))...  119 us
    reduce_scatter x1, waiting for transfers between devices, shards(): lax.psum_scatter(picked.astype(jnp.float32).astype(jnp.bfloat16), 'group'...  33.3 us
    psum x1, blocking collectives, shards(): coefficients = lax.psum(partial_value, 'tensor')  5.75 us
  transfers between devices with their start and end apart: 1, of which 1 were waited for; matrix products, arithmetic and copies ran while one was open for 0% of the time, Pallas kernels for 0%

profile of v1, /device:TPU:2, one launch (start us, length us, event | category | flops | bytes accessed | tf_op | source)
XLA Modules:
  0.0 178.3 jit_solution(14444260581980952074)
XLA Ops:
  7.2 0.0 copy-start
  7.2 0.0 reduce-scatter.2.cloned.1.call-start
  7.2 1.5 copy-done
  8.8 0.6 dynamic-slice_bitcast_fusion
  9.4 0.0 reduce-scatter.2.cloned.1.call-update
  9.4 33.3 %reduce-scatter.2.cloned.1.call-done = bf16[1,16,512]{2,1,0:T(8,128)(2,1)} async-done(((bf16[4,16,512]{2,1,0:T(8,128)(2,1)}), bf16[1,16,512]{2,1,0:T(8,128)(2,1)}) %reduce-scatter.2.cloned.1.call-update) | async-done | bytes 16400 | tf_op jit(solution)/shard_map/reduce_scatter | solution.py:20
  42.7 1.0 fusion
  43.7 5.7 %psum.7 = f32[16,64]{1,0:T(8,128)S(1)} all-reduce(f32[16,64]{1,0:T(8,128)S(1)} %fusion), channel_id=1, replica_groups=mesh['group'=4,'shard'=32,'tensor'=4] {'tensor'}, use_global_device_ids=true, to_apply=%region_1.2 | all-reduce | flops 1024 | bytes 8192 | tf_op jit(solution)/shard_map/psum | solution.py:24
  49.4 1.6 fusion.2
  51.1 0.2 stack.2
  51.3 118.8 %all_to_all.5 = bf16[128,16,512]{2,1,0:T(8,128)(2,1)S(1)} all-to-all(bf16[128,16,512]{2,1,0:T(8,128)(2,1)S(1)} %stack.2), channel_id=1, replica_groups=mesh['group'=4,'shard'=32,'tensor'=4] {'group','shard'}, dimensions={0} | all-to-all | bytes 4194304 | tf_op jit(solution)/shard_map/all_to_all | solution.py:35
  170.1 1.3 copy.8
Async XLA Ops:
  7.2 1.6 copy-start
  7.2 35.5 %reduce-scatter.2.cloned.1.call-start = ((), (), s32[]{:S(2)}) async-start(), calls=%async_computation.2 | async-start | bytes 81920 | tf_op jit(solution)/shard_map/reduce_scatter | solution.py:20
Sparse Core Ops, SparseCore 0:
  11.4 31.2 reduce-scatter.1
